TPU v7x, 128 devices: a whole 4x4x4 slice. The times are simulated.
128 devices in a mesh: dp: 32 (over y, x, core), tensor: 4 (over z).
Axes of the slice: x: 4, y: 4, z: 4, core: 2. Of those that a mesh axis runs over, the one named last changes fastest.
Arguments:
- tokens: bfloat16 [20480, 1152], P(('dp', 'tensor')), may hold values from -6 to 6
- cotangent: bfloat16 [20480, 1152], P(('dp', 'tensor')), may hold values from -24 to 24
- segment_ids: int32 [32, 640], P('dp'), may hold values from 0 to 3, as said below
- positions: int32 [32, 640], P('dp'), may hold values from 0 to 1999, as said below
- w_query: bfloat16 [1152, 1024], P('dp', 'tensor')
- w_key: bfloat16 [1152, 256], P('dp')
- w_value: bfloat16 [1152, 256], P('dp'), may hold values from -0.1875 to 0.1875
- w_out: bfloat16 [1024, 1152], P('tensor', 'dp'), may hold values from -0.1875 to 0.1875
- w_gate: bfloat16 [1152, 6912], P('dp', 'tensor'), may hold values from -0.1875 to 0.1875
- w_up: bfloat16 [1152, 6912], P('dp', 'tensor'), may hold values from -0.1875 to 0.1875
- w_down: bfloat16 [6912, 1152], P('tensor', 'dp'), may hold values from -0.078125 to 0.078125
- prenorm_attn: bfloat16 [1152], P('dp'), may hold values from 0.099609375 to 1.8984375
- postnorm_attn: bfloat16 [1152], P('dp'), may hold values from 0.099609375 to 1.8984375
- prenorm_ffw: bfloat16 [1152], P('dp'), may hold values from 0.099609375 to 1.8984375
- postnorm_ffw: bfloat16 [1152], P('dp'), may hold values from 0.099609375 to 1.8984375
- query_norm: bfloat16 [256], P('dp'), may hold values from 0.6 to 5
- key_norm: bfloat16 [256], P('dp'), may hold values from 0.6 to 5
Outputs:
- layer_out: bfloat16 [20480, 1152], P(('dp', 'tensor'))
- grad_tokens: float32 [20480, 1152], P(('dp', 'tensor'))
- grad_query: float32 [1152, 1024], P('dp', 'tensor')
- grad_key: float32 [1152, 256], P('dp')
- grad_value: float32 [1152, 256], P('dp')
- grad_output: float32 [1024, 1152], P('tensor', 'dp')
- grad_gate: float32 [1152, 6912], P('dp', 'tensor')
- grad_up: float32 [1152, 6912], P('dp', 'tensor')
- grad_down: float32 [6912, 1152], P('tensor', 'dp')
- grad_prenorm_attn: float32 [1152], P('dp')
- grad_postnorm_attn: float32 [1152], P('dp')
- grad_prenorm_ffw: float32 [1152], P('dp')
- grad_postnorm_ffw: float32 [1152], P('dp')
- grad_query_norm: float32 [256], P('dp')
- grad_key_norm: float32 [256], P('dp')
Inputs may be any that keep to these rules, and one draw needn't show every extreme that they name: `segment_ids`: within each sequence the numbers never fall; a document is a run of equal numbers. Within a document positions rise by one from token to token.
All inputs are finite; a program needn't handle non-finite values.
Results may differ from a plain program's by a relative error of at most 0.033.
The roundings to bfloat16 on the way count: a program that leaves them out, or rounds other values in their place, can miss the bound.
Values may be sent and summed in bfloat16 or wider, within the bound.
A program may use at most 128 MiB of HBM per device.

v0:
```python
import math
import jax
import jax.numpy as jnp
from jax import lax
from jax.sharding import PartitionSpec as P

WINDOW = 512
EPSILON = 1e-06
ROPE_BASE = 10000.0
GELU_SCALE = math.sqrt(2.0 / math.pi)
MASKED = -1e30


def normalize(inputs):
    inverse = lax.rsqrt(jnp.mean(inputs * inputs, axis=-1, keepdims=True) + EPSILON)
    return (inputs * inverse, inverse)


def normalize_back(grad_hat, normed, inverse):
    return inverse * (grad_hat - normed * jnp.mean(grad_hat * normed, axis=-1, keepdims=True))


def rotary_tables(places, width):
    half = width // 2
    freqs = ROPE_BASE ** (-(jnp.arange(half, dtype=jnp.float32) * 2.0) / width)
    angles = places.astype(jnp.float32)[:, None] * freqs[None, :]
    return (jnp.cos(angles), jnp.sin(angles))


def rotate(inputs, cosine, sine):
    half = inputs.shape[-1] // 2
    first = inputs[:, :half]
    second = inputs[:, half:]
    return jnp.concatenate(
        [first * cosine - second * sine, second * cosine + first * sine], axis=-1
    )


def gelu_parts(inputs):
    inner = GELU_SCALE * (inputs + 0.044715 * inputs * inputs * inputs)
    tangent = jnp.tanh(inner)
    result = 0.5 * inputs * (1.0 + tangent)
    slope = 0.5 * (1.0 + tangent) + 0.5 * inputs * (1.0 - tangent * tangent) * GELU_SCALE * (
        1.0 + 3.0 * 0.044715 * inputs * inputs
    )
    return (result, slope)


def window_mask(segments):
    length = segments.shape[0]
    places = jnp.arange(length, dtype=jnp.int32)
    offset = places[:, None] - places[None, :]
    same = segments[:, None] == segments[None, :]
    return same & (offset >= 0) & (offset < WINDOW)


def contract_rows(left, right):
    return lax.dot_general(
        left, right, (((0,), (0,)), ((), ())), preferred_element_type=jnp.float32
    )


def contract_cols(left, right):
    return lax.dot_general(
        left, right, (((1,), (1,)), ((), ())), preferred_element_type=jnp.float32
    )


def attend_scores(queries, keys, allowed, scale):
    return jnp.where(allowed, contract_cols(queries, keys) * scale, MASKED)


def attend_forward(queries, keys, values, allowed, scale):
    scores = attend_scores(queries, keys, allowed, scale)
    top = jnp.max(scores, axis=-1, keepdims=True)
    totals = jnp.sum(jnp.exp(scores - top), axis=-1, keepdims=True)
    logsum = top + jnp.log(totals)
    probs = jnp.exp(scores - logsum).astype(jnp.bfloat16)
    return (jnp.dot(probs, values, preferred_element_type=jnp.float32), logsum)


def attend_backward(queries, keys, values, allowed, scale, logsum, grad_heads):
    probs = jnp.exp(attend_scores(queries, keys, allowed, scale) - logsum)
    grad_values = contract_rows(probs.astype(jnp.bfloat16), grad_heads)
    grad_probs = contract_cols(grad_heads, values)
    centre = jnp.sum(probs * grad_probs, axis=-1, keepdims=True)
    grad_scores = (probs * (grad_probs - centre) * scale).astype(jnp.bfloat16)
    grad_queries = jnp.dot(grad_scores, keys, preferred_element_type=jnp.float32)
    grad_keys = contract_rows(grad_scores, queries)
    return (grad_queries, grad_keys, grad_values)


def local(
    tokens,
    cotangent,
    segment_ids,
    positions,
    w_query,
    w_key,
    w_value,
    w_out,
    w_gate,
    w_up,
    w_down,
    prenorm_attn,
    postnorm_attn,
    prenorm_ffw,
    postnorm_ffw,
    query_norm,
    key_norm,
):
    residual = tokens.astype(jnp.float32)
    attn_mats = (
        lax.all_gather(w_query, "dp", axis=0, tiled=True),
        lax.all_gather(w_key, "dp", axis=0, tiled=True),
        lax.all_gather(w_value, "dp", axis=0, tiled=True),
        lax.all_gather(w_out, "dp", axis=1, tiled=True),
        lax.all_gather(prenorm_attn, "dp", axis=0, tiled=True),
        lax.all_gather(postnorm_attn, "dp", axis=0, tiled=True),
        lax.all_gather(query_norm, "dp", axis=0, tiled=True),
        lax.all_gather(key_norm, "dp", axis=0, tiled=True),
    )
    full_query, full_key, full_value, full_out = (
        attn_mats[0],
        attn_mats[1],
        attn_mats[2],
        attn_mats[3],
    )
    gain_in = attn_mats[4].astype(jnp.float32)
    gain_post = attn_mats[5].astype(jnp.float32)
    gain_query = attn_mats[6].astype(jnp.float32)
    gain_key = attn_mats[7].astype(jnp.float32)
    normed_in, inverse_in = normalize(residual)
    attn_rows = lax.all_gather(
        (normed_in * gain_in).astype(jnp.bfloat16), "tensor", axis=0, tiled=True
    )
    width = full_key.shape[1]
    scale = 1.0 / math.sqrt(width)
    cosine, sine = rotary_tables(positions.reshape(-1), width)
    masks = [window_mask(segment_ids[0])]
    key_hat, key_inverse = normalize(
        jnp.dot(attn_rows, full_key, preferred_element_type=jnp.float32)
    )
    keys = rotate(key_hat * gain_key, cosine, sine).astype(jnp.bfloat16)
    values = jnp.dot(attn_rows, full_value, preferred_element_type=jnp.float32).astype(jnp.bfloat16)
    query_hat, query_inverse = normalize(
        jnp.dot(attn_rows, full_query, preferred_element_type=jnp.float32)
    )
    queries = rotate(query_hat * gain_query, cosine, sine).astype(jnp.bfloat16)
    sequence = 0
    piece, logsum = attend_forward(queries, keys, values, masks[sequence], scale)
    logsums = logsum
    saved = [(query_hat, query_inverse, queries, logsums)]
    heads_out = piece.astype(jnp.bfloat16)
    attn_sum = lax.psum_scatter(
        jnp.dot(heads_out, full_out, preferred_element_type=jnp.float32),
        "tensor",
        scatter_dimension=0,
        tiled=True,
    )
    attn_hat, attn_inverse = normalize(attn_sum)
    hidden = residual + attn_hat * gain_post
    ffw_mats = (
        lax.all_gather(w_gate, "dp", axis=0, tiled=True),
        lax.all_gather(w_up, "dp", axis=0, tiled=True),
        lax.all_gather(w_down, "dp", axis=1, tiled=True),
        lax.all_gather(prenorm_ffw, "dp", axis=0, tiled=True),
        lax.all_gather(postnorm_ffw, "dp", axis=0, tiled=True),
    )
    full_gate, full_up, full_down = (ffw_mats[0], ffw_mats[1], ffw_mats[2])
    gain_ffw_in = ffw_mats[3].astype(jnp.float32)
    gain_ffw_post = ffw_mats[4].astype(jnp.float32)
    mid_hat, mid_inverse = normalize(hidden)
    ffw_rows = lax.all_gather(
        (mid_hat * gain_ffw_in).astype(jnp.bfloat16), "tensor", axis=0, tiled=True
    )
    gate = jnp.dot(ffw_rows, full_gate, preferred_element_type=jnp.float32)
    upward = jnp.dot(ffw_rows, full_up, preferred_element_type=jnp.float32)
    gelu_value, gelu_slope = gelu_parts(gate)
    act = (gelu_value * upward).astype(jnp.bfloat16)
    ffw_sum = lax.psum_scatter(
        jnp.dot(act, full_down, preferred_element_type=jnp.float32),
        "tensor",
        scatter_dimension=0,
        tiled=True,
    )
    ffw_hat, ffw_inverse = normalize(ffw_sum)
    layer_out = (hidden + ffw_hat * gain_ffw_post).astype(jnp.bfloat16)
    back_mats = (
        lax.all_gather(w_query, "dp", axis=0, tiled=True),
        lax.all_gather(w_key, "dp", axis=0, tiled=True),
        lax.all_gather(w_value, "dp", axis=0, tiled=True),
        lax.all_gather(w_out, "dp", axis=1, tiled=True),
        lax.all_gather(w_gate, "dp", axis=0, tiled=True),
        lax.all_gather(w_up, "dp", axis=0, tiled=True),
        lax.all_gather(w_down, "dp", axis=1, tiled=True),
    )
    back_query, back_key, back_value, back_out = (
        back_mats[0],
        back_mats[1],
        back_mats[2],
        back_mats[3],
    )
    back_gate, back_up, back_down = (back_mats[4], back_mats[5], back_mats[6])
    grad_out = cotangent.astype(jnp.float32)
    grad_post_ffw = jnp.sum(grad_out * ffw_hat, axis=0)
    grad_ffw_local = normalize_back(grad_out * gain_ffw_post, ffw_hat, ffw_inverse).astype(
        jnp.bfloat16
    )
    grad_ffw = lax.all_gather(grad_ffw_local, "tensor", axis=0, tiled=True)
    grad_down_turned = contract_rows(grad_ffw, act)
    grad_act = contract_cols(grad_ffw, back_down)
    grad_gate_in = (grad_act * upward * gelu_slope).astype(jnp.bfloat16)
    grad_up_in = (grad_act * gelu_value).astype(jnp.bfloat16)
    grad_gate = contract_rows(ffw_rows, grad_gate_in)
    grad_up = contract_rows(ffw_rows, grad_up_in)
    ffw_in_shards = (
        lax.psum_scatter(
            grad_gate.astype(jnp.bfloat16), "dp", scatter_dimension=0, tiled=True
        ).astype(jnp.float32),
        lax.psum_scatter(
            grad_up.astype(jnp.bfloat16), "dp", scatter_dimension=0, tiled=True
        ).astype(jnp.float32),
    )
    grad_mid = lax.psum_scatter(
        contract_cols(grad_gate_in, back_gate) + contract_cols(grad_up_in, back_up),
        "tensor",
        scatter_dimension=0,
        tiled=True,
    )
    grad_pre_ffw = jnp.sum(grad_mid * mid_hat, axis=0)
    grad_hidden = grad_out + normalize_back(grad_mid * gain_ffw_in, mid_hat, mid_inverse)
    grad_post_attn = jnp.sum(grad_hidden * attn_hat, axis=0)
    grad_attn_local = normalize_back(grad_hidden * gain_post, attn_hat, attn_inverse).astype(
        jnp.bfloat16
    )
    grad_attn = lax.all_gather(grad_attn_local, "tensor", axis=0, tiled=True)
    grad_out_turned = contract_rows(grad_attn, heads_out)
    grad_heads = contract_cols(grad_attn, back_out).astype(jnp.bfloat16)
    which = 0
    query_hat, query_inverse, queries, logsum = saved[which]
    sequence = 0
    grad_queries, grad_keys, grad_values = attend_backward(
        queries, keys, values, masks[sequence], scale, logsum, grad_heads
    )
    grad_query_turned = rotate(grad_queries, cosine, -sine)
    grad_query_norm = jnp.sum(grad_query_turned * query_hat, axis=0)
    query_in = normalize_back(grad_query_turned * gain_query, query_hat, query_inverse).astype(
        jnp.bfloat16
    )
    grad_key_turned = rotate(grad_keys, cosine, -sine)
    grad_key_norm = jnp.sum(grad_key_turned * key_hat, axis=0)
    key_in = normalize_back(grad_key_turned * gain_key, key_hat, key_inverse).astype(jnp.bfloat16)
    value_in = grad_values.astype(jnp.bfloat16)
    query_blocks = contract_rows(attn_rows, query_in)
    grad_key = contract_rows(attn_rows, key_in)
    grad_value = contract_rows(attn_rows, value_in)
    query_ins = [query_in]
    key_ins = [key_in]
    value_ins = [value_in]
    which = 0
    total = contract_cols(query_ins[which], back_query)
    total = total + contract_cols(key_ins[which], back_key)
    total = total + contract_cols(value_ins[which], back_value)
    grad_in_rows = lax.psum_scatter(
        total.astype(jnp.bfloat16), "tensor", scatter_dimension=0, tiled=True
    ).astype(jnp.float32)
    grad_pre_attn = jnp.sum(grad_in_rows * normed_in, axis=0)
    grad_tokens = grad_hidden + normalize_back(grad_in_rows * gain_in, normed_in, inverse_in)
    rest = (
        lax.psum_scatter(
            query_blocks.astype(jnp.bfloat16), "dp", scatter_dimension=0, tiled=True
        ).astype(jnp.float32),
        lax.psum_scatter(
            grad_key.astype(jnp.bfloat16), "dp", scatter_dimension=0, tiled=True
        ).astype(jnp.float32),
        lax.psum_scatter(
            grad_value.astype(jnp.bfloat16), "dp", scatter_dimension=0, tiled=True
        ).astype(jnp.float32),
        lax.psum_scatter(
            grad_out_turned.astype(jnp.bfloat16), "dp", scatter_dimension=0, tiled=True
        ).astype(jnp.float32),
        lax.psum_scatter(
            grad_down_turned.astype(jnp.bfloat16), "dp", scatter_dimension=0, tiled=True
        ).astype(jnp.float32),
        lax.psum_scatter(
            grad_pre_attn.astype(jnp.bfloat16), "dp", scatter_dimension=0, tiled=True
        ).astype(jnp.float32),
        lax.psum_scatter(
            grad_post_attn.astype(jnp.bfloat16), "dp", scatter_dimension=0, tiled=True
        ).astype(jnp.float32),
        lax.psum_scatter(
            grad_pre_ffw.astype(jnp.bfloat16), "dp", scatter_dimension=0, tiled=True
        ).astype(jnp.float32),
        lax.psum_scatter(
            grad_post_ffw.astype(jnp.bfloat16), "dp", scatter_dimension=0, tiled=True
        ).astype(jnp.float32),
        lax.psum_scatter(
            grad_query_norm.astype(jnp.bfloat16), "dp", scatter_dimension=0, tiled=True
        ).astype(jnp.float32),
        lax.psum_scatter(
            grad_key_norm.astype(jnp.bfloat16), "dp", scatter_dimension=0, tiled=True
        ).astype(jnp.float32),
    )
    shared = (
        lax.psum(rest[1].astype(jnp.bfloat16), "tensor").astype(jnp.float32),
        lax.psum(rest[2].astype(jnp.bfloat16), "tensor").astype(jnp.float32),
        lax.psum(rest[5].astype(jnp.bfloat16), "tensor").astype(jnp.float32),
        lax.psum(rest[6].astype(jnp.bfloat16), "tensor").astype(jnp.float32),
        lax.psum(rest[7].astype(jnp.bfloat16), "tensor").astype(jnp.float32),
        lax.psum(rest[8].astype(jnp.bfloat16), "tensor").astype(jnp.float32),
        lax.psum(rest[9].astype(jnp.bfloat16), "tensor").astype(jnp.float32),
        lax.psum(rest[10].astype(jnp.bfloat16), "tensor").astype(jnp.float32),
    )
    return (
        layer_out,
        grad_tokens,
        rest[0],
        shared[0],
        shared[1],
        rest[3].T,
        ffw_in_shards[0],
        ffw_in_shards[1],
        rest[4].T,
        shared[2],
        shared[3],
        shared[4],
        shared[5],
        shared[6],
        shared[7],
    )


def solution(mesh):
    placed = (
        P(("dp", "tensor"), None),
        P(("dp", "tensor"), None),
        P("dp", None),
        P("dp", None),
        P("dp", "tensor"),
        P("dp", None),
        P("dp", None),
        P("tensor", "dp"),
        P("dp", "tensor"),
        P("dp", "tensor"),
        P("tensor", "dp"),
        P("dp"),
        P("dp"),
        P("dp"),
        P("dp"),
        P("dp"),
        P("dp"),
    )
    return jax.shard_map(
        local,
        mesh=mesh,
        in_specs=placed,
        out_specs=(
            P(("dp", "tensor"), None),
            P(("dp", "tensor"), None),
            P("dp", "tensor"),
            P("dp", None),
            P("dp", None),
            P("tensor", "dp"),
            P("dp", "tensor"),
            P("dp", "tensor"),
            P("tensor", "dp"),
            P("dp"),
            P("dp"),
            P("dp"),
            P("dp"),
            P("dp"),
            P("dp"),
        ),
        check_vma=False,
    )
```

profile of v0, /device:TPU:0, one launch (start us, length us, event | category | flops | bytes accessed | tf_op | source)
XLA Modules:
  0.0 971.6 jit_solution(9938166193788936195)
XLA Ops:
  15.8 128.5 %all-reduce.27 = (bf16[1152]{0:T(1024)(128)(2,1)S(1)}, bf16[256]{0:T(256)(128)(2,1)S(1)}, bf16[256]{0:T(256)(128)(2,1)S(1)}, bf16[1152]{0:T(1024)(128)(2,1)S(1)}...) all-reduce(bf16[1152]{0:T(1024)(128)(2,1)S(1)} %dynamic-update-slic, ...), channel_id=1, replica_groups=mesh['dp'=32,'tensor'=4] {'dp'}, use_global_device_ids=true, to_apply=%add | all-reduce | flops 5120 | bytes 20480
  147.5 22.5 %all-gather.2 = bf16[32,36,256]{2,1,0:T(8,128)(2,1)S(1)} all-gather(bf16[1,36,256]{2,1,0:T(8,128)(2,1)} %bitcast.84), channel_id=1, replica_groups=mesh['dp'=32,'tensor'=4] {'dp'}, dimensions={0}, use_global_device_ids=true | all-gather | bytes 608256 | tf_op jit(solution)/shard_map/all_gather | solution.py:116
  170.2 24.3 %all-gather.1 = bf16[32,36,256]{2,1,0:T(8,128)(2,1)S(1)} all-gather(bf16[1,36,256]{2,1,0:T(8,128)(2,1)S(1)} %bitcast.85), channel_id=1, replica_groups=mesh['dp'=32,'tensor'=4] {'dp'}, dimensions={0}, use_global_device_ids=true | all-gather | bytes 608256 | tf_op jit(solution)/shard_map/all_gather | solution.py:115
  194.7 22.6 %all-gather = bf16[32,36,256]{2,1,0:T(8,128)(2,1)S(1)} all-gather(bf16[1,36,256]{2,1,0:T(8,128)(2,1)S(1)} %bitcast.86), channel_id=1, replica_groups=mesh['dp'=32,'tensor'=4] {'dp'}, dimensions={0}, use_global_device_ids=true | all-gather | bytes 608256 | tf_op jit(solution)/shard_map/all_gather | solution.py:114
  217.5 24.6 %all-gather.3 = bf16[32,36,256]{2,1,0:T(8,128)(2,1)S(1)} all-gather(bf16[1,36,256]{2,1,0:T(8,128)(2,1)S(1)} %bitcast.87), channel_id=1, replica_groups=mesh['dp'=32,'tensor'=4] {'dp'}, dimensions={0}, use_global_device_ids=true | all-gather | bytes 608256 | tf_op jit(solution)/shard_map/all_gather | solution.py:117
  254.9 34.6 %reduce-scatter.19.cloned.1.call-done = f32[160,1152]{1,0:T(8,128)} async-done(((f32[640,1152]{1,0:T(8,128)}), f32[160,1152]{1,0:T(8,128)}) %reduce-scatter.19.cloned.1.call-update) | async-done | bytes 737296 | tf_op jit(solution)/shard_map/reduce_scatter | solution.py:155
  293.6 8.0 all-gather.23.cloned.1.call-done
  301.6 7.3 reshape.160
  308.9 40.7 %all-gather.25.cloned.1.call-done = bf16[32,36,1728]{2,1,0:T(8,128)(2,1)} async-done(((bf16[1,36,1728]{2,1,0:T(8,128)(2,1)}), bf16[32,36,1728]{2,1,0:T(8,128)(2,1)}) %all-gather.25.cloned.1.call-update) | async-done | bytes 3981328 | tf_op jit(solution)/shard_map/all_gather | solution.py:165
  349.5 7.3 reshape.162
  356.8 40.7 %all-gather.27.cloned.1.call-done = bf16[32,36,1728]{2,1,0:T(8,128)(2,1)} async-done(((bf16[1,36,1728]{2,1,0:T(8,128)(2,1)}), bf16[32,36,1728]{2,1,0:T(8,128)(2,1)}) %all-gather.27.cloned.1.call-update) | async-done | bytes 3981328 | tf_op jit(solution)/shard_map/all_gather | solution.py:166
  397.5 7.3 reshape.164
  404.8 20.2 %all-gather.17.cloned.1.call-done = bf16[640,1152]{1,0:T(8,128)(2,1)} async-done(((bf16[160,1152]{1,0:T(8,128)(2,1)}), bf16[640,1152]{1,0:T(8,128)(2,1)}) %all-gather.17.cloned.1.call-update) | async-done | bytes 1474576 | tf_op jit(solution)/shard_map/all_gather | solution.py:174
  425.0 6.5 fusion.77
  431.5 6.7 multiply_convert_fusion.1
  439.7 4.8 fusion.78
  444.7 36.9 %reduce-scatter.21.cloned.1.call-done = f32[160,1152]{1,0:T(8,128)} async-done(((f32[640,1152]{1,0:T(8,128)}), f32[160,1152]{1,0:T(8,128)}) %reduce-scatter.21.cloned.1.call-update) | async-done | bytes 737296 | tf_op jit(solution)/shard_map/reduce_scatter | solution.py:181
  485.6 25.6 %all-gather.19.cloned.1.call-done = bf16[640,1152]{1,0:T(8,128)(2,1)} async-done(((bf16[160,1152]{1,0:T(8,128)(2,1)}), bf16[640,1152]{1,0:T(8,128)(2,1)}) %all-gather.19.cloned.1.call-update) | async-done | bytes 1474576 | tf_op jit(solution)/shard_map/all_gather | solution.py:210
  511.2 10.2 %multiply_convert_fusion = (bf16[640,1728]{0,1:T(8,128)(2,1)S(1)}, bf16[640,1728]{0,1:T(8,128)(2,1)S(1)}) fusion(f32[640,1728]{0,1:T(8,128)} %copy-done.52, f32[640,1728]{0,1:T(8,128)} %get-tuple-element.90, bf16[640,1152]{1,0:T(8,128)(2,1)} %all-gather.19.cloned.1.call-done, bf16[1152,1728]{1,0:T(8,128)(2,1)} %reshape.164), kind=kOutput, calls=%fused_computation.12 | convolution fusion | flops 2573475840 | bytes 18726912 | tf_op jit(solution)/shard_map/dot_general | solution.py:64
  521.5 3.2 fusion.79
  525.2 4.9 convolution_add_fusion.2
  530.2 37.1 %reduce-scatter.23.cloned.1.call-done = f32[160,1152]{1,0:T(8,128)} async-done(((f32[640,1152]{1,0:T(8,128)}), f32[160,1152]{1,0:T(8,128)}) %reduce-scatter.23.cloned.1.call-update) | async-done | bytes 737296 | tf_op jit(solution)/shard_map/reduce_scatter | solution.py:225
  572.7 7.7 convolution_convert_fusion.2
  580.4 5.4 convolution_convert_fusion.1
  585.8 12.3 %all-gather.21.cloned.1.call-done = bf16[640,1152]{1,0:T(8,128)(2,1)} async-done(((bf16[160,1152]{1,0:T(8,128)(2,1)}), bf16[640,1152]{1,0:T(8,128)(2,1)}) %all-gather.21.cloned.1.call-update) | async-done | bytes 1474576 | tf_op jit(solution)/shard_map/all_gather | solution.py:237
  610.4 7.6 convolution_convert_fusion
  623.2 98.4 %fusion.73 = (bf16[40,256]{1,0:T(8,128)(2,1)S(1)}, bf16[40,256]{1,0:T(8,128)(2,1)S(1)}, bf16[40,256]{1,0:T(8,128)(2,1)S(1)}, bf16[40,256]{1,0:T(8,128)(2,1)S(1)}...) fusion(bf16[1152,256]{1,0:T(8,128)(2,1)S(1)} %convolution_convert_fusion.6, ...), kind=kCustom, calls=%all-reduce-scatter.7 | all-reduce-scatter fusion | flops 7946241 | bytes 14800384
  724.3 5.6 collective-permute-start.23
  732.1 5.3 collective-permute-start.7
  737.5 3.0 collective-permute-start.11
  740.5 5.2 collective-permute-start.15
  749.1 5.1 collective-permute-start.6
  754.3 4.0 collective-permute-start.5
  759.8 3.3 collective-permute-start.10
  763.1 3.7 collective-permute-start.9
  766.8 2.5 collective-permute-start.14
  769.4 3.6 collective-permute-start.13
  773.1 2.3 collective-permute-start.12
  778.4 2.5 collective-permute-start.8
  782.9 2.5 collective-permute-start.17
  787.1 2.4 collective-permute-start.22
  794.0 2.5 collective-permute-start.20
  798.0 2.9 collective-permute-start.25
  800.9 2.4 collective-permute-start.24
  806.4 2.5 concatenate.23
  809.4 3.2 concatenate.24
  816.3 123.9 %all-reduce.26 = (bf16[1152]{0:T(1024)(128)(2,1)S(1)}, bf16[1152]{0:T(1024)(128)(2,1)S(1)}, bf16[1152]{0:T(1024)(128)(2,1)S(1)}, bf16[1152]{0:T(1024)(128)(2,1)S...) all-reduce(bf16[1152]{0:T(1024)(128)(2,1)S(1)} %get-tuple-element.2, ...), channel_id=13, replica_groups=mesh['dp'=32,'tensor'=4] {'dp'}, use_global_device_ids=true, to_apply=%region_29.30.clone | all-reduce | flops 5120 | bytes 20480
  940.7 16.3 %all-reduce.28 = (bf16[36,256]{1,0:T(8,128)(2,1)S(1)}, bf16[36,256]{1,0:T(8,128)(2,1)S(1)}, bf16[36]{0:T(256)(128)(2,1)S(1)}, bf16[36]{0:T(256)(128)(2,1)S(1)}, ...) all-reduce(bf16[36,256]{1,0:T(8,128)(2,1)S(1)} %constant_dynamic-sl, ...), channel_id=1, replica_groups=mesh['dp'=32,'tensor'=4] {'tensor'}, use_global_device_ids=true, to_apply=%region_21.22 | all-reduce | flops 18592 | bytes 74368 | tf_op jit(solution)/shard_map/psum | solution.py:306
  (289 shorter events, 90.0 us)
Async XLA Ops:
  8.0 162.2 %copy-start.38 = (bf16[36,256]{1,0:T(8,128)(2,1)S(1)}, bf16[36,256]{1,0:T(8,128)(2,1)}, u32[]{:S(2)}) copy-start(bf16[36,256]{1,0:T(8,128)(2,1)} %param.22) | copy-start | bytes 55300
  8.0 234.3 %all-gather.15.cloned.1.call-start = ((), (), s32[]{:S(2)}) async-start(), calls=%async_computation.4 | async-start | bytes 1843200 | tf_op jit(solution)/shard_map/all_gather | solution.py:134
  147.4 47.3 %copy-start.39 = (bf16[36,256]{1,0:T(8,128)(2,1)S(1)}, bf16[36,256]{1,0:T(8,128)(2,1)}, u32[]{:S(2)}) copy-start(bf16[36,256]{1,0:T(8,128)(2,1)} %param.21) | copy-start | bytes 55300
  147.5 142.0 %reduce-scatter.19.cloned.1.call-start = ((), (), s32[]{:S(2)}) async-start(), calls=%async_computation.5 | async-start | bytes 3686400 | tf_op jit(solution)/shard_map/reduce_scatter | solution.py:155
  170.2 78.1 %copy-start.20 = (bf16[1152,256]{1,0:T(8,128)(2,1)}, bf16[1152,256]{1,0:T(8,128)(2,1)S(1)}, u32[]{:S(2)}) copy-start(bf16[1152,256]{1,0:T(8,128)(2,1)S(1)} %reshape.156) | copy-start | bytes 1769476
  170.2 47.3 %copy-start.40 = (bf16[256,36]{0,1:T(8,128)(2,1)S(1)}, bf16[256,36]{0,1:T(8,128)(2,1)}, u32[]{:S(2)}) copy-start(bf16[256,36]{0,1:T(8,128)(2,1)} %param.24) | copy-start | bytes 55300
  194.6 49.9 %copy-start.11 = (bf16[1152,256]{1,0:T(8,128)(2,1)}, bf16[1152,256]{1,0:T(8,128)(2,1)S(1)}, u32[]{:S(2)}) copy-start(bf16[1152,256]{1,0:T(8,128)(2,1)S(1)} %reshape.154) | copy-start | bytes 1769476
  194.7 47.5 %copy-start.44 = (s32[1,640]{1,0:T(1,128)S(1)}, s32[1,640]{1,0:T(1,128)}, u32[]{:S(2)}) copy-start(s32[1,640]{1,0:T(1,128)} %param.19) | copy-start | bytes 7684
  194.7 47.6 %copy-start.45 = (s32[1,640]{1,0:T(1,128)S(1)}, s32[1,640]{1,0:T(1,128)}, u32[]{:S(2)}) copy-start(s32[1,640]{1,0:T(1,128)} %param.20) | copy-start | bytes 7684
  194.7 50.7 %copy-start.42 = (f32[256]{0:T(256)}, f32[256]{0:T(256)S(1)}, u32[]{:S(2)}) copy-start(f32[256]{0:T(256)S(1)} %convert_element_type.184) | copy-start | bytes 3076
  253.1 48.5 %all-gather.23.cloned.1.call-start = ((), (), s32[]{:S(2)}) async-start(), calls=%async_computation.12 | async-start | bytes 4730880 | tf_op jit(solution)/shard_map/all_gather | solution.py:164
  253.6 95.9 %all-gather.25.cloned.1.call-start = ((), (), s32[]{:S(2)}) async-start(), calls=%async_computation.13 | async-start | bytes 4730880 | tf_op jit(solution)/shard_map/all_gather | solution.py:165
  254.2 143.3 %all-gather.27.cloned.1.call-start = ((), (), s32[]{:S(2)}) async-start(), calls=%async_computation.14 | async-start | bytes 4730880 | tf_op jit(solution)/shard_map/all_gather | solution.py:166
  254.8 170.2 %all-gather.17.cloned.1.call-start = ((), (), s32[]{:S(2)}) async-start(), calls=%async_computation.6 | async-start | bytes 1843200 | tf_op jit(solution)/shard_map/all_gather | solution.py:174
  293.1 188.5 %reduce-scatter.21.cloned.1.call-start = ((), (), s32[]{:S(2)}) async-start(), calls=%async_computation.7 | async-start | bytes 3686400 | tf_op jit(solution)/shard_map/reduce_scatter | solution.py:181
  444.5 66.7 %all-gather.19.cloned.1.call-start = ((), (), s32[]{:S(2)}) async-start(), calls=%async_computation.8 | async-start | bytes 1843200 | tf_op jit(solution)/shard_map/all_gather | solution.py:210
  485.6 81.7 %reduce-scatter.23.cloned.1.call-start = ((), (), s32[]{:S(2)}) async-start(), calls=%async_computation.9 | async-start | bytes 3686400 | tf_op jit(solution)/shard_map/reduce_scatter | solution.py:225
  530.2 67.8 %all-gather.21.cloned.1.call-start = ((), (), s32[]{:S(2)}) async-start(), calls=%async_computation.10 | async-start | bytes 1843200 | tf_op jit(solution)/shard_map/all_gather | solution.py:237
  572.4 242.5 %reduce-scatter.25.cloned.1.call-start = ((), (), s32[]{:S(2)}) async-start(), calls=%async_computation.11 | async-start | bytes 1843200 | tf_op jit(solution)/shard_map/reduce_scatter | solution.py:265
  721.7 36.6 %collective-permute-start.2 = (bf16[40,256]{1,0:T(8,128)(2,1)S(1)}, bf16[40,256]{1,0:T(8,128)(2,1)S(1)}, u32[]{:S(2)}, u32[]{:S(2)}) collective-permute-start(bf16[40,256]{1,0:T(8,128)(2,1)S(1)} %get-tuple-element.54), channel_id=1, source_target_pairs={{0,12},{4,16},{8,20},{12,24},{16,28},{20,32},{24,36},{28,40},{32,4... | collective-permute-start | bytes 61448
  723.0 26.1 %collective-permute-start.19 = (bf16[4,1728]{1,0:T(4,128)(2,1)S(1)}, bf16[4,1728]{1,0:T(4,128)(2,1)S(1)}, u32[]{:S(2)}, u32[]{:S(2)}) collective-permute-start(bf16[4,1728]{1,0:T(4,128)(2,1)S(1)} %slice.44), channel_id=1, source_target_pairs={{0,16},{4,20},{8,24},{12,28},{16,32},{20,36},{24,40},{28,44},{32,4... | collective-permute-start | bytes 41480
  724.3 30.0 %collective-permute-start.23 = (bf16[4,1728]{1,0:T(4,128)(2,1)S(1)}, bf16[4,1728]{1,0:T(4,128)(2,1)}, u32[]{:S(2)}, u32[]{:S(2)}) collective-permute-start(bf16[4,1728]{1,0:T(4,128)(2,1)S(1)} %slice.45), channel_id=1, source_target_pairs={{0,16},{4,20},{8,24},{12,28},{16,32},{20,36},{24,40},{28,44},{32,4... | collective-permute-start | bytes 41480
  730.0 7.5 collective-permute-start.3
  732.1 8.3 collective-permute-start.7
  737.5 8.3 collective-permute-start.11
  740.5 6.5 collective-permute-start.15
  745.7 14.1 %collective-permute-start.1 = (bf16[40,256]{1,0:T(8,128)(2,1)S(1)}, bf16[40,256]{1,0:T(8,128)(2,1)S(1)}, u32[]{:S(2)}, u32[]{:S(2)}) collective-permute-start(bf16[40,256]{1,0:T(8,128)(2,1)S(1)} %get-tuple-element.54), channel_id=1, source_target_pairs={{0,8},{4,12},{8,16},{12,20},{16,24},{20,28},{24,32},{28,36},{32,40... | collective-permute-start | bytes 61448
  747.0 16.1 %collective-permute-start = (bf16[40,256]{1,0:T(8,128)(2,1)S(1)}, bf16[40,256]{1,0:T(8,128)(2,1)S(1)}, u32[]{:S(2)}, u32[]{:S(2)}) collective-permute-start(bf16[40,256]{1,0:T(8,128)(2,1)S(1)} %get-tuple-element.54), channel_id=1, source_target_pairs={{0,4},{4,8},{8,12},{12,16},{16,20},{20,24},{24,28},{28,32},{32,36}... | collective-permute-start | bytes 61448
  749.1 17.7 %collective-permute-start.6 = (bf16[40,256]{1,0:T(8,128)(2,1)S(1)}, bf16[40,256]{1,0:T(8,128)(2,1)S(1)}, u32[]{:S(2)}, u32[]{:S(2)}) collective-permute-start(bf16[40,256]{1,0:T(8,128)(2,1)S(1)} %get-tuple-element.55), channel_id=1, source_target_pairs={{0,12},{4,16},{8,20},{12,24},{16,28},{20,32},{24,36},{28,40},{32,4... | collective-permute-start | bytes 61448
  754.3 15.1 %collective-permute-start.5 = (bf16[40,256]{1,0:T(8,128)(2,1)S(1)}, bf16[40,256]{1,0:T(8,128)(2,1)S(1)}, u32[]{:S(2)}, u32[]{:S(2)}) collective-permute-start(bf16[40,256]{1,0:T(8,128)(2,1)S(1)} %get-tuple-element.55), channel_id=1, source_target_pairs={{0,8},{4,12},{8,16},{12,20},{16,24},{20,28},{24,32},{28,36},{32,40... | collective-permute-start | bytes 61448
  758.3 14.8 %collective-permute-start.4 = (bf16[40,256]{1,0:T(8,128)(2,1)S(1)}, bf16[40,256]{1,0:T(8,128)(2,1)S(1)}, u32[]{:S(2)}, u32[]{:S(2)}) collective-permute-start(bf16[40,256]{1,0:T(8,128)(2,1)S(1)} %get-tuple-element.55), channel_id=1, source_target_pairs={{0,4},{4,8},{8,12},{12,16},{16,20},{20,24},{24,28},{28,32},{32,36}... | collective-permute-start | bytes 61448
  759.8 18.7 %collective-permute-start.10 = (bf16[40,256]{1,0:T(8,128)(2,1)S(1)}, bf16[40,256]{1,0:T(8,128)(2,1)S(1)}, u32[]{:S(2)}, u32[]{:S(2)}) collective-permute-start(bf16[40,256]{1,0:T(8,128)(2,1)S(1)} %get-tuple-element.56), channel_id=1, source_target_pairs={{0,12},{4,16},{8,20},{12,24},{16,28},{20,32},{24,36},{28,40},{32,4... | collective-permute-start | bytes 61448
  763.1 17.8 %collective-permute-start.9 = (bf16[40,256]{1,0:T(8,128)(2,1)S(1)}, bf16[40,256]{1,0:T(8,128)(2,1)S(1)}, u32[]{:S(2)}, u32[]{:S(2)}) collective-permute-start(bf16[40,256]{1,0:T(8,128)(2,1)S(1)} %get-tuple-element.56), channel_id=1, source_target_pairs={{0,8},{4,12},{8,16},{12,20},{16,24},{20,28},{24,32},{28,36},{32,40... | collective-permute-start | bytes 61448
  766.8 16.0 %collective-permute-start.14 = (bf16[40,256]{1,0:T(8,128)(2,1)S(1)}, bf16[40,256]{1,0:T(8,128)(2,1)S(1)}, u32[]{:S(2)}, u32[]{:S(2)}) collective-permute-start(bf16[40,256]{1,0:T(8,128)(2,1)S(1)} %get-tuple-element.57), channel_id=1, source_target_pairs={{0,12},{4,16},{8,20},{12,24},{16,28},{20,32},{24,36},{28,40},{32,4... | collective-permute-start | bytes 61448
  769.4 16.0 %collective-permute-start.13 = (bf16[40,256]{1,0:T(8,128)(2,1)S(1)}, bf16[40,256]{1,0:T(8,128)(2,1)S(1)}, u32[]{:S(2)}, u32[]{:S(2)}) collective-permute-start(bf16[40,256]{1,0:T(8,128)(2,1)S(1)} %get-tuple-element.57), channel_id=1, source_target_pairs={{0,8},{4,12},{8,16},{12,20},{16,24},{20,28},{24,32},{28,36},{32,40... | collective-permute-start | bytes 61448
  773.1 14.1 %collective-permute-start.12 = (bf16[40,256]{1,0:T(8,128)(2,1)S(1)}, bf16[40,256]{1,0:T(8,128)(2,1)S(1)}, u32[]{:S(2)}, u32[]{:S(2)}) collective-permute-start(bf16[40,256]{1,0:T(8,128)(2,1)S(1)} %get-tuple-element.57), channel_id=1, source_target_pairs={{0,4},{4,8},{8,12},{12,16},{16,20},{20,24},{24,28},{28,32},{32,36}... | collective-permute-start | bytes 61448
  778.4 12.2 %collective-permute-start.8 = (bf16[40,256]{1,0:T(8,128)(2,1)S(1)}, bf16[40,256]{1,0:T(8,128)(2,1)S(1)}, u32[]{:S(2)}, u32[]{:S(2)}) collective-permute-start(bf16[40,256]{1,0:T(8,128)(2,1)S(1)} %get-tuple-element.56), channel_id=1, source_target_pairs={{0,4},{4,8},{8,12},{12,16},{16,20},{20,24},{24,28},{28,32},{32,36}... | collective-permute-start | bytes 61448
  781.0 13.0 %collective-permute-start.18 = (bf16[40,1728]{1,0:T(8,128)(2,1)S(1)}, bf16[40,1728]{1,0:T(8,128)(2,1)S(1)}, u32[]{:S(2)}, u32[]{:S(2)}) collective-permute-start(bf16[40,1728]{1,0:T(8,128)(2,1)S(1)} %get-tuple-element.58), channel_id=1, source_target_pairs={{0,12},{4,16},{8,20},{12,24},{16,28},{20,32},{24,36},{28,40},{32,4... | collective-permute-start | bytes 414728
  782.9 13.6 %collective-permute-start.17 = (bf16[40,1728]{1,0:T(8,128)(2,1)S(1)}, bf16[40,1728]{1,0:T(8,128)(2,1)S(1)}, u32[]{:S(2)}, u32[]{:S(2)}) collective-permute-start(bf16[40,1728]{1,0:T(8,128)(2,1)S(1)} %get-tuple-element.58), channel_id=1, source_target_pairs={{0,8},{4,12},{8,16},{12,20},{16,24},{20,28},{24,32},{28,36},{32,40... | collective-permute-start | bytes 414728
  785.4 12.6 %collective-permute-start.16 = (bf16[40,1728]{1,0:T(8,128)(2,1)S(1)}, bf16[40,1728]{1,0:T(8,128)(2,1)S(1)}, u32[]{:S(2)}, u32[]{:S(2)}) collective-permute-start(bf16[40,1728]{1,0:T(8,128)(2,1)S(1)} %get-tuple-element.58), channel_id=1, source_target_pairs={{0,4},{4,8},{8,12},{12,16},{16,20},{20,24},{24,28},{28,32},{32,36}... | collective-permute-start | bytes 414728
  787.1 13.7 %collective-permute-start.22 = (bf16[40,1728]{1,0:T(8,128)(2,1)S(1)}, bf16[40,1728]{1,0:T(8,128)(2,1)S(1)}, u32[]{:S(2)}, u32[]{:S(2)}) collective-permute-start(bf16[40,1728]{1,0:T(8,128)(2,1)S(1)} %get-tuple-element.59), channel_id=1, source_target_pairs={{0,12},{4,16},{8,20},{12,24},{16,28},{20,32},{24,36},{28,40},{32,4... | collective-permute-start | bytes 414728
  790.7 13.4 %collective-permute-start.21 = (bf16[40,1728]{1,0:T(8,128)(2,1)S(1)}, bf16[40,1728]{1,0:T(8,128)(2,1)S(1)}, u32[]{:S(2)}, u32[]{:S(2)}) collective-permute-start(bf16[40,1728]{1,0:T(8,128)(2,1)S(1)} %get-tuple-element.59), channel_id=1, source_target_pairs={{0,8},{4,12},{8,16},{12,20},{16,24},{20,28},{24,32},{28,36},{32,40... | collective-permute-start | bytes 414728
  794.0 12.4 %collective-permute-start.20 = (bf16[40,1728]{1,0:T(8,128)(2,1)S(1)}, bf16[40,1728]{1,0:T(8,128)(2,1)}, u32[]{:S(2)}, u32[]{:S(2)}) collective-permute-start(bf16[40,1728]{1,0:T(8,128)(2,1)S(1)} %get-tuple-element.59), channel_id=1, source_target_pairs={{0,4},{4,8},{8,12},{12,16},{16,20},{20,24},{24,28},{28,32},{32,36}... | collective-permute-start | bytes 414728
  796.5 12.3 %collective-permute-start.26 = (bf16[40,1728]{1,0:T(8,128)(2,1)S(1)}, bf16[40,1728]{1,0:T(8,128)(2,1)S(1)}, u32[]{:S(2)}, u32[]{:S(2)}) collective-permute-start(bf16[40,1728]{1,0:T(8,128)(2,1)S(1)} %get-tuple-element.60), channel_id=1, source_target_pairs={{0,12},{4,16},{8,20},{12,24},{16,28},{20,32},{24,36},{28,40},{32,4... | collective-permute-start | bytes 414728
  798.0 10.9 %collective-permute-start.25 = (bf16[40,1728]{1,0:T(8,128)(2,1)S(1)}, bf16[40,1728]{1,0:T(8,128)(2,1)}, u32[]{:S(2)}, u32[]{:S(2)}) collective-permute-start(bf16[40,1728]{1,0:T(8,128)(2,1)S(1)} %get-tuple-element.60), channel_id=1, source_target_pairs={{0,8},{4,12},{8,16},{12,20},{16,24},{20,28},{24,32},{28,36},{32,40... | collective-permute-start | bytes 414728
  800.9 8.6 collective-permute-start.24
  804.1 4.7 collective-permute-start.27
  806.3 155.0 %copy-start.7 = (f32[160,1152]{1,0:T(8,128)S(1)}, f32[160,1152]{1,0:T(8,128)}, u32[]{:S(2)}) copy-start(f32[160,1152]{1,0:T(8,128)} %copy-done.6) | copy-start | bytes 2211844
  (48 other events, 307.0 us)
Sparse Core Ops, SparseCore 0:
  147.6 23.1 all-gather.14
  253.2 36.2 reduce-scatter.18
  444.6 36.9 reduce-scatter.20
  485.7 25.4 all-gather.18
  530.3 36.9 reduce-scatter.22
  572.5 25.4 all-gather.20
  610.5 25.3 reduce-scatter.24
Sparse Core Ops, SparseCore 1:
  255.9 45.7 all-gather.22
  303.8 45.7 all-gather.24
  351.7 45.7 all-gather.26
  399.8 25.1 all-gather.16
where the time goes:
time: 980 us; the launch traced here: 972 us
  blocking collectives  461 us (47%)
  waiting for transfers between devices  258 us (26%)
  starting transfers between devices  78.2 us (8%)
  matrix products  76 us (8%)
  local copies, waits for them, and re-layouts  45.5 us (5%)
  other arithmetic  32 us (3%)
  between operations  21 us (2%)
    unnamed x3, blocking collectives  351 us
    unnamed x28, starting transfers between devices  76.9 us
    unnamed x156, local copies, waits for them, and re-layouts  45.5 us
    all_gather x1, waiting for transfers between devices, local(): lax.all_gather(w_down, 'dp', axis=1, tiled=True)  40.7 us
    all_gather x1, waiting for transfers between devices, local(): lax.all_gather(w_up, 'dp', axis=0, tiled=True)  40.7 us
    reduce_scatter x1, waiting for transfers between devices, local(): lax.psum_scatter(contract_cols(grad_gate_in, back_gate) + contract_cols(g...  37.1 us
    reduce_scatter x1, waiting for transfers between devices, local(): lax.psum_scatter(jnp.dot(act, full_down, preferred_element_type=jnp.float...  36.9 us
    reduce_scatter x1, waiting for transfers between devices, local(): lax.psum_scatter(jnp.dot(heads_out, full_out, preferred_element_type=jnp....  34.6 us
  transfers between devices with their start and end apart: 39, of which 9 were waited for; matrix products, arithmetic and copies ran while one was open for 17% of the time, Pallas kernels for 0%

commit v1 on v0

--- a/solution.py
+++ b/solution.py
@@ -9,6 +9,28 @@
 ROPE_BASE = 10000.0
 GELU_SCALE = math.sqrt(2.0 / math.pi)
 MASKED = -1e30
+
+
+def laid_out(tiles, dim):
+    shape = list(tiles.shape[1:])
+    shape[dim] *= tiles.shape[0]
+    return jnp.moveaxis(tiles, 0, dim).reshape(shape)
+
+
+def gather_around(x, axis, dim):
+    size = lax.axis_size(axis)
+    pairs = [(i, (i + 1) % size) for i in range(size)]
+    back = [(b, a) for a, b in pairs]
+    lower, upper = ([], [])
+    for lap in range(size - 1):
+        if lap % 2 == 0:
+            lower.append(lax.ppermute(lower[-1] if lower else x, axis, pairs))
+        else:
+            upper.append(lax.ppermute(upper[-1] if upper else x, axis, back))
+    pieces = jnp.stack([*lower[::-1], x, *upper])
+    shift = lax.axis_index(axis) - len(lower)
+    pieces = pieces[(jnp.arange(size) - shift) % size]
+    return laid_out(pieces, dim)
 
 
 def normalize(inputs):
@@ -171,9 +193,7 @@
     gain_ffw_in = ffw_mats[3].astype(jnp.float32)
     gain_ffw_post = ffw_mats[4].astype(jnp.float32)
     mid_hat, mid_inverse = normalize(hidden)
-    ffw_rows = lax.all_gather(
-        (mid_hat * gain_ffw_in).astype(jnp.bfloat16), "tensor", axis=0, tiled=True
-    )
+    ffw_rows = gather_around((mid_hat * gain_ffw_in).astype(jnp.bfloat16), "tensor", 0)
     gate = jnp.dot(ffw_rows, full_gate, preferred_element_type=jnp.float32)
     upward = jnp.dot(ffw_rows, full_up, preferred_element_type=jnp.float32)
     gelu_value, gelu_slope = gelu_parts(gate)

time: 980 us -> 976 us (level)
  waiting for transfers between devices: 258 us -> 247 us
    all_gather x1 -> x0, waiting for transfers between devices: 20.2 us -> none  [local(): lax.all_gather((mid_hat * gain_ffw_in).astype(jnp.bfloat16), 'tensor', ax...]
    ppermute x0 -> x3, waiting for transfers between devices: none -> 11.5 us  [the longest x1 7.7 us: gather_around(): upper.append(lax.ppermute(upper[-1] if upper else x, axis, back))]
  transfers between devices with their start and end apart: 39 -> 41, of which waited for: 9 -> 10; matrix products, arithmetic and copies ran while one was open for 17% -> 17% of each run, Pallas kernels for 0% -> 0%
where the time goes in v1:
time: 976 us; the launch traced here: 968 us
  blocking collectives  461 us (47%)
  waiting for transfers between devices  247 us (25%)
  starting transfers between devices  81.3 us (8%)
  matrix products  76.1 us (8%)
  local copies, waits for them, and re-layouts  48.8 us (5%)
  other arithmetic  32.7 us (3%)
  between operations  21 us (2%)
    unnamed x3, blocking collectives  351 us
    unnamed x28, starting transfers between devices  77 us
    unnamed x156, local copies, waits for them, and re-layouts  45.6 us
    all_gather x1, waiting for transfers between devices, local(): lax.all_gather(w_down, 'dp', axis=1, tiled=True)  40.7 us
    all_gather x1, waiting for transfers between devices, local(): lax.all_gather(w_up, 'dp', axis=0, tiled=True)  40.7 us
    reduce_scatter x1, waiting for transfers between devices, local(): lax.psum_scatter(contract_cols(grad_gate_in, back_gate) + contract_cols(g...  37.1 us
    reduce_scatter x1, waiting for transfers between devices, local(): lax.psum_scatter(jnp.dot(heads_out, full_out, preferred_element_type=jnp....  34.6 us
    reduce_scatter x1, waiting for transfers between devices, local(): lax.psum_scatter(jnp.dot(act, full_down, preferred_element_type=jnp.float...  33.6 us
  transfers between devices with their start and end apart: 41, of which 10 were waited for; matrix products, arithmetic and copies ran while one was open for 17% of the time, Pallas kernels for 0%

profile of v1, /device:TPU:0, one launch (start us, length us, event | category | flops | bytes accessed | tf_op | source)
XLA Modules:
  0.0 968.0 jit_solution(5206081704763167617)
XLA Ops:
  15.8 128.5 %all-reduce.27 = (bf16[1152]{0:T(1024)(128)(2,1)S(1)}, bf16[256]{0:T(256)(128)(2,1)S(1)}, bf16[256]{0:T(256)(128)(2,1)S(1)}, bf16[1152]{0:T(1024)(128)(2,1)S(1)}...) all-reduce(bf16[1152]{0:T(1024)(128)(2,1)S(1)} %dynamic-update-slic, ...), channel_id=1, replica_groups=mesh['dp'=32,'tensor'=4] {'dp'}, use_global_device_ids=true, to_apply=%add | all-reduce | flops 5120 | bytes 20480
  147.5 22.5 %all-gather.2 = bf16[32,36,256]{2,1,0:T(8,128)(2,1)S(1)} all-gather(bf16[1,36,256]{2,1,0:T(8,128)(2,1)} %bitcast.99), channel_id=1, replica_groups=mesh['dp'=32,'tensor'=4] {'dp'}, dimensions={0}, use_global_device_ids=true | all-gather | bytes 608256 | tf_op jit(solution)/shard_map/all_gather | solution.py:138
  170.2 24.3 %all-gather.1 = bf16[32,36,256]{2,1,0:T(8,128)(2,1)S(1)} all-gather(bf16[1,36,256]{2,1,0:T(8,128)(2,1)S(1)} %bitcast.100), channel_id=1, replica_groups=mesh['dp'=32,'tensor'=4] {'dp'}, dimensions={0}, use_global_device_ids=true | all-gather | bytes 608256 | tf_op jit(solution)/shard_map/all_gather | solution.py:137
  194.7 22.6 %all-gather = bf16[32,36,256]{2,1,0:T(8,128)(2,1)S(1)} all-gather(bf16[1,36,256]{2,1,0:T(8,128)(2,1)S(1)} %bitcast.101), channel_id=1, replica_groups=mesh['dp'=32,'tensor'=4] {'dp'}, dimensions={0}, use_global_device_ids=true | all-gather | bytes 608256 | tf_op jit(solution)/shard_map/all_gather | solution.py:136
  217.5 24.6 %all-gather.3 = bf16[32,36,256]{2,1,0:T(8,128)(2,1)S(1)} all-gather(bf16[1,36,256]{2,1,0:T(8,128)(2,1)S(1)} %bitcast.102), channel_id=1, replica_groups=mesh['dp'=32,'tensor'=4] {'dp'}, dimensions={0}, use_global_device_ids=true | all-gather | bytes 608256 | tf_op jit(solution)/shard_map/all_gather | solution.py:139
  254.9 34.6 %reduce-scatter.19.cloned.1.call-done = f32[160,1152]{1,0:T(8,128)} async-done(((f32[640,1152]{1,0:T(8,128)}), f32[160,1152]{1,0:T(8,128)}) %reduce-scatter.19.cloned.1.call-update) | async-done | bytes 737296 | tf_op jit(solution)/shard_map/reduce_scatter | solution.py:177
  292.6 9.0 all-gather.20.cloned.1.call-done
  301.6 7.3 reshape.221
  308.9 40.7 %all-gather.22.cloned.1.call-done = bf16[32,36,1728]{2,1,0:T(8,128)(2,1)} async-done(((bf16[1,36,1728]{2,1,0:T(8,128)(2,1)}), bf16[32,36,1728]{2,1,0:T(8,128)(2,1)}) %all-gather.22.cloned.1.call-update) | async-done | bytes 3981328 | tf_op jit(solution)/shard_map/all_gather | solution.py:187
  349.6 7.3 reshape.223
  356.8 40.7 %all-gather.24.cloned.1.call-done = bf16[32,36,1728]{2,1,0:T(8,128)(2,1)} async-done(((bf16[1,36,1728]{2,1,0:T(8,128)(2,1)}), bf16[32,36,1728]{2,1,0:T(8,128)(2,1)}) %all-gather.24.cloned.1.call-update) | async-done | bytes 3981328 | tf_op jit(solution)/shard_map/all_gather | solution.py:188
  397.5 7.3 reshape.225
  404.8 2.9 collective-permute-start.2
  408.3 7.7 collective-permute-done.2
  416.0 3.8 collective-permute-done.1
  421.2 3.2 gather_fusion
  424.4 6.5 fusion.79
  431.0 6.7 multiply_convert_fusion.1
  439.1 4.8 fusion.80
  444.2 33.6 %reduce-scatter.21.cloned.1.call-done = f32[160,1152]{1,0:T(8,128)} async-done(((f32[640,1152]{1,0:T(8,128)}), f32[160,1152]{1,0:T(8,128)}) %reduce-scatter.21.cloned.1.call-update) | async-done | bytes 737296 | tf_op jit(solution)/shard_map/reduce_scatter | solution.py:201
  481.9 25.6 %all-gather.16.cloned.1.call-done = bf16[640,1152]{1,0:T(8,128)(2,1)} async-done(((bf16[160,1152]{1,0:T(8,128)(2,1)}), bf16[640,1152]{1,0:T(8,128)(2,1)}) %all-gather.16.cloned.1.call-update) | async-done | bytes 1474576 | tf_op jit(solution)/shard_map/all_gather | solution.py:230
  507.5 10.2 %multiply_convert_fusion = (bf16[640,1728]{0,1:T(8,128)(2,1)S(1)}, bf16[640,1728]{0,1:T(8,128)(2,1)S(1)}) fusion(f32[640,1728]{0,1:T(8,128)} %copy-done.52, f32[640,1728]{0,1:T(8,128)} %get-tuple-element.90, bf16[640,1152]{1,0:T(8,128)(2,1)} %all-gather.16.cloned.1.call-done, bf16[1152,1728]{1,0:T(8,128)(2,1)} %reshape.225), kind=kOutput, calls=%fused_computation.13 | convolution fusion | flops 2573475840 | bytes 18726912 | tf_op jit(solution)/shard_map/dot_general | solution.py:86
  517.8 3.2 fusion.81
  521.5 4.9 convolution_add_fusion.2
  526.5 37.1 %reduce-scatter.23.cloned.1.call-done = f32[160,1152]{1,0:T(8,128)} async-done(((f32[640,1152]{1,0:T(8,128)}), f32[160,1152]{1,0:T(8,128)}) %reduce-scatter.23.cloned.1.call-update) | async-done | bytes 737296 | tf_op jit(solution)/shard_map/reduce_scatter | solution.py:245
  568.9 7.6 convolution_convert_fusion.2
  576.5 5.4 convolution_convert_fusion.1
  581.9 12.3 %all-gather.18.cloned.1.call-done = bf16[640,1152]{1,0:T(8,128)(2,1)} async-done(((bf16[160,1152]{1,0:T(8,128)(2,1)}), bf16[640,1152]{1,0:T(8,128)(2,1)}) %all-gather.18.cloned.1.call-update) | async-done | bytes 1474576 | tf_op jit(solution)/shard_map/all_gather | solution.py:257
  606.7 7.6 convolution_convert_fusion
  619.6 98.4 %fusion.75 = (bf16[40,256]{1,0:T(8,128)(2,1)S(1)}, bf16[40,256]{1,0:T(8,128)(2,1)S(1)}, bf16[40,256]{1,0:T(8,128)(2,1)S(1)}, bf16[40,256]{1,0:T(8,128)(2,1)S(1)}...) fusion(bf16[1152,256]{1,0:T(8,128)(2,1)S(1)} %convolution_convert_fusion.6, ...), kind=kCustom, calls=%all-reduce-scatter.7 | all-reduce-scatter fusion | flops 7946241 | bytes 14800384
  720.7 5.6 collective-permute-start.26
  728.5 5.3 collective-permute-start.10
  733.8 3.0 collective-permute-start.14
  736.9 5.2 collective-permute-start.18
  745.5 5.1 collective-permute-start.9
  750.7 4.0 collective-permute-start.8
  756.2 3.3 collective-permute-start.13
  759.5 3.7 collective-permute-start.12
  763.2 2.5 collective-permute-start.17
  765.8 3.7 collective-permute-start.16
  774.8 2.5 collective-permute-start.11
  779.3 2.5 collective-permute-start.20
  790.4 2.5 collective-permute-start.23
  794.4 2.9 collective-permute-start.28
  802.8 2.5 concatenate.23
  805.8 3.2 concatenate.24
  812.7 123.9 %all-reduce.26 = (bf16[1152]{0:T(1024)(128)(2,1)S(1)}, bf16[1152]{0:T(1024)(128)(2,1)S(1)}, bf16[1152]{0:T(1024)(128)(2,1)S(1)}, bf16[1152]{0:T(1024)(128)(2,1)S...) all-reduce(bf16[1152]{0:T(1024)(128)(2,1)S(1)} %get-tuple-element.2, ...), channel_id=13, replica_groups=mesh['dp'=32,'tensor'=4] {'dp'}, use_global_device_ids=true, to_apply=%region_29.30.clone | all-reduce | flops 5120 | bytes 20480
  937.0 16.3 %all-reduce.28 = (bf16[36,256]{1,0:T(8,128)(2,1)S(1)}, bf16[36,256]{1,0:T(8,128)(2,1)S(1)}, bf16[36]{0:T(256)(128)(2,1)S(1)}, bf16[36]{0:T(256)(128)(2,1)S(1)}, ...) all-reduce(bf16[36,256]{1,0:T(8,128)(2,1)S(1)} %constant_dynamic-sl, ...), channel_id=1, replica_groups=mesh['dp'=32,'tensor'=4] {'tensor'}, use_global_device_ids=true, to_apply=%region_21.22 | all-reduce | flops 18592 | bytes 74368 | tf_op jit(solution)/shard_map/psum | solution.py:326
  (297 shorter events, 98.1 us)
Async XLA Ops:
  8.0 162.2 %copy-start.40 = (bf16[36,256]{1,0:T(8,128)(2,1)S(1)}, bf16[36,256]{1,0:T(8,128)(2,1)}, u32[]{:S(2)}) copy-start(bf16[36,256]{1,0:T(8,128)(2,1)} %param.22) | copy-start | bytes 55300
  8.0 234.3 %all-gather.14.cloned.1.call-start = ((), (), s32[]{:S(2)}) async-start(), calls=%async_computation.4 | async-start | bytes 1843200 | tf_op jit(solution)/shard_map/all_gather | solution.py:156
  147.5 142.0 %reduce-scatter.19.cloned.1.call-start = ((), (), s32[]{:S(2)}) async-start(), calls=%async_computation.5 | async-start | bytes 3686400 | tf_op jit(solution)/shard_map/reduce_scatter | solution.py:177
  170.2 78.1 %copy-start.20 = (bf16[1152,256]{1,0:T(8,128)(2,1)}, bf16[1152,256]{1,0:T(8,128)(2,1)S(1)}, u32[]{:S(2)}) copy-start(bf16[1152,256]{1,0:T(8,128)(2,1)S(1)} %reshape.217) | copy-start | bytes 1769476
  194.6 49.9 %copy-start.11 = (bf16[1152,256]{1,0:T(8,128)(2,1)}, bf16[1152,256]{1,0:T(8,128)(2,1)S(1)}, u32[]{:S(2)}) copy-start(bf16[1152,256]{1,0:T(8,128)(2,1)S(1)} %reshape.215) | copy-start | bytes 1769476
  194.7 47.5 %copy-start.46 = (s32[1,640]{1,0:T(1,128)S(1)}, s32[1,640]{1,0:T(1,128)}, u32[]{:S(2)}) copy-start(s32[1,640]{1,0:T(1,128)} %param.19) | copy-start | bytes 7684
  194.7 47.6 %copy-start.47 = (s32[1,640]{1,0:T(1,128)S(1)}, s32[1,640]{1,0:T(1,128)}, u32[]{:S(2)}) copy-start(s32[1,640]{1,0:T(1,128)} %param.20) | copy-start | bytes 7684
  194.7 50.7 %copy-start.44 = (f32[256]{0:T(256)}, f32[256]{0:T(256)S(1)}, u32[]{:S(2)}) copy-start(f32[256]{0:T(256)S(1)} %convert_element_type.184) | copy-start | bytes 3076
  253.1 48.5 %all-gather.20.cloned.1.call-start = ((), (), s32[]{:S(2)}) async-start(), calls=%async_computation.11 | async-start | bytes 4730880 | tf_op jit(solution)/shard_map/all_gather | solution.py:186
  253.6 95.9 %all-gather.22.cloned.1.call-start = ((), (), s32[]{:S(2)}) async-start(), calls=%async_computation.12 | async-start | bytes 4730880 | tf_op jit(solution)/shard_map/all_gather | solution.py:187
  254.2 143.3 %all-gather.24.cloned.1.call-start = ((), (), s32[]{:S(2)}) async-start(), calls=%async_computation.13 | async-start | bytes 4730880 | tf_op jit(solution)/shard_map/all_gather | solution.py:188
  254.8 223.1 %reduce-scatter.21.cloned.1.call-start = ((), (), s32[]{:S(2)}) async-start(), calls=%async_computation.6 | async-start | bytes 3686400 | tf_op jit(solution)/shard_map/reduce_scatter | solution.py:201
  292.4 115.4 %collective-permute-start = (bf16[160,1152]{1,0:T(8,128)(2,1)S(1)}, bf16[160,1152]{1,0:T(8,128)(2,1)S(1)}, u32[]{:S(2)}, u32[]{:S(2)}) collective-permute-start(bf16[160,1152]{1,0:T(8,128)(2,1)S(1)} %multiply_convert_fusion.4), channel_id=1, source_target_pairs={{0,1},{1,2},{2,3},{3,0},{4,5},{5,6},{6,7},{7,4},{8,9},{9,10},{10,1... | collective-permute-start | bytes 1105928 | tf_op jit(solution)/shard_map/ppermute | solution.py:27
  404.8 11.2 %collective-permute-start.2 = (bf16[160,1152]{1,0:T(8,128)(2,1)S(1)}, bf16[160,1152]{1,0:T(8,128)(2,1)S(1)}, u32[]{:S(2)}, u32[]{:S(2)}) collective-permute-start(bf16[160,1152]{1,0:T(8,128)(2,1)S(1)} %multiply_convert_fusion.4), channel_id=1, source_target_pairs={{1,0},{2,1},{3,2},{0,3},{5,4},{6,5},{7,6},{4,7},{9,8},{10,9},{11,1... | collective-permute-start | bytes 1105928 | tf_op jit(solution)/shard_map/ppermute | solution.py:29
  407.8 12.0 %collective-permute-start.1 = (bf16[160,1152]{1,0:T(8,128)(2,1)S(1)}, bf16[160,1152]{1,0:T(8,128)(2,1)S(1)}, u32[]{:S(2)}, u32[]{:S(2)}) collective-permute-start(bf16[160,1152]{1,0:T(8,128)(2,1)S(1)} %collective-permute-done), channel_id=1, source_target_pairs={{0,1},{1,2},{2,3},{3,0},{4,5},{5,6},{6,7},{7,4},{8,9},{9,10},{10,1... | collective-permute-start | bytes 1105928 | tf_op jit(solution)/shard_map/ppermute | solution.py:27
  444.0 63.5 %all-gather.16.cloned.1.call-start = ((), (), s32[]{:S(2)}) async-start(), calls=%async_computation.7 | async-start | bytes 1843200 | tf_op jit(solution)/shard_map/all_gather | solution.py:230
  481.9 81.7 %reduce-scatter.23.cloned.1.call-start = ((), (), s32[]{:S(2)}) async-start(), calls=%async_computation.8 | async-start | bytes 3686400 | tf_op jit(solution)/shard_map/reduce_scatter | solution.py:245
  526.4 67.8 %all-gather.18.cloned.1.call-start = ((), (), s32[]{:S(2)}) async-start(), calls=%async_computation.9 | async-start | bytes 1843200 | tf_op jit(solution)/shard_map/all_gather | solution.py:257
  568.6 242.7 %reduce-scatter.25.cloned.1.call-start = ((), (), s32[]{:S(2)}) async-start(), calls=%async_computation.10 | async-start | bytes 1843200 | tf_op jit(solution)/shard_map/reduce_scatter | solution.py:285
  718.1 36.6 %collective-permute-start.5 = (bf16[40,256]{1,0:T(8,128)(2,1)S(1)}, bf16[40,256]{1,0:T(8,128)(2,1)S(1)}, u32[]{:S(2)}, u32[]{:S(2)}) collective-permute-start(bf16[40,256]{1,0:T(8,128)(2,1)S(1)} %get-tuple-element.54), channel_id=1, source_target_pairs={{0,12},{4,16},{8,20},{12,24},{16,28},{20,32},{24,36},{28,40},{32,4... | collective-permute-start | bytes 61448
  719.4 26.1 %collective-permute-start.22 = (bf16[4,1728]{1,0:T(4,128)(2,1)S(1)}, bf16[4,1728]{1,0:T(4,128)(2,1)S(1)}, u32[]{:S(2)}, u32[]{:S(2)}) collective-permute-start(bf16[4,1728]{1,0:T(4,128)(2,1)S(1)} %slice.46), channel_id=1, source_target_pairs={{0,16},{4,20},{8,24},{12,28},{16,32},{20,36},{24,40},{28,44},{32,4... | collective-permute-start | bytes 41480
  720.7 30.0 %collective-permute-start.26 = (bf16[4,1728]{1,0:T(4,128)(2,1)S(1)}, bf16[4,1728]{1,0:T(4,128)(2,1)}, u32[]{:S(2)}, u32[]{:S(2)}) collective-permute-start(bf16[4,1728]{1,0:T(4,128)(2,1)S(1)} %slice.47), channel_id=1, source_target_pairs={{0,16},{4,20},{8,24},{12,28},{16,32},{20,36},{24,40},{28,44},{32,4... | collective-permute-start | bytes 41480
  726.3 7.5 collective-permute-start.6
  728.5 8.3 collective-permute-start.10
  733.8 8.2 collective-permute-start.14
  736.9 6.5 collective-permute-start.18
  742.1 14.1 %collective-permute-start.4 = (bf16[40,256]{1,0:T(8,128)(2,1)S(1)}, bf16[40,256]{1,0:T(8,128)(2,1)S(1)}, u32[]{:S(2)}, u32[]{:S(2)}) collective-permute-start(bf16[40,256]{1,0:T(8,128)(2,1)S(1)} %get-tuple-element.54), channel_id=1, source_target_pairs={{0,8},{4,12},{8,16},{12,20},{16,24},{20,28},{24,32},{28,36},{32,40... | collective-permute-start | bytes 61448
  743.4 16.1 %collective-permute-start.3 = (bf16[40,256]{1,0:T(8,128)(2,1)S(1)}, bf16[40,256]{1,0:T(8,128)(2,1)S(1)}, u32[]{:S(2)}, u32[]{:S(2)}) collective-permute-start(bf16[40,256]{1,0:T(8,128)(2,1)S(1)} %get-tuple-element.54), channel_id=1, source_target_pairs={{0,4},{4,8},{8,12},{12,16},{16,20},{20,24},{24,28},{28,32},{32,36}... | collective-permute-start | bytes 61448
  745.5 17.7 %collective-permute-start.9 = (bf16[40,256]{1,0:T(8,128)(2,1)S(1)}, bf16[40,256]{1,0:T(8,128)(2,1)S(1)}, u32[]{:S(2)}, u32[]{:S(2)}) collective-permute-start(bf16[40,256]{1,0:T(8,128)(2,1)S(1)} %get-tuple-element.55), channel_id=1, source_target_pairs={{0,12},{4,16},{8,20},{12,24},{16,28},{20,32},{24,36},{28,40},{32,4... | collective-permute-start | bytes 61448
  750.7 15.1 %collective-permute-start.8 = (bf16[40,256]{1,0:T(8,128)(2,1)S(1)}, bf16[40,256]{1,0:T(8,128)(2,1)S(1)}, u32[]{:S(2)}, u32[]{:S(2)}) collective-permute-start(bf16[40,256]{1,0:T(8,128)(2,1)S(1)} %get-tuple-element.55), channel_id=1, source_target_pairs={{0,8},{4,12},{8,16},{12,20},{16,24},{20,28},{24,32},{28,36},{32,40... | collective-permute-start | bytes 61448
  754.7 14.8 %collective-permute-start.7 = (bf16[40,256]{1,0:T(8,128)(2,1)S(1)}, bf16[40,256]{1,0:T(8,128)(2,1)S(1)}, u32[]{:S(2)}, u32[]{:S(2)}) collective-permute-start(bf16[40,256]{1,0:T(8,128)(2,1)S(1)} %get-tuple-element.55), channel_id=1, source_target_pairs={{0,4},{4,8},{8,12},{12,16},{16,20},{20,24},{24,28},{28,32},{32,36}... | collective-permute-start | bytes 61448
  756.2 18.7 %collective-permute-start.13 = (bf16[40,256]{1,0:T(8,128)(2,1)S(1)}, bf16[40,256]{1,0:T(8,128)(2,1)S(1)}, u32[]{:S(2)}, u32[]{:S(2)}) collective-permute-start(bf16[40,256]{1,0:T(8,128)(2,1)S(1)} %get-tuple-element.56), channel_id=1, source_target_pairs={{0,12},{4,16},{8,20},{12,24},{16,28},{20,32},{24,36},{28,40},{32,4... | collective-permute-start | bytes 61448
  759.5 17.9 %collective-permute-start.12 = (bf16[40,256]{1,0:T(8,128)(2,1)S(1)}, bf16[40,256]{1,0:T(8,128)(2,1)S(1)}, u32[]{:S(2)}, u32[]{:S(2)}) collective-permute-start(bf16[40,256]{1,0:T(8,128)(2,1)S(1)} %get-tuple-element.56), channel_id=1, source_target_pairs={{0,8},{4,12},{8,16},{12,20},{16,24},{20,28},{24,32},{28,36},{32,40... | collective-permute-start | bytes 61448
  763.2 16.1 %collective-permute-start.17 = (bf16[40,256]{1,0:T(8,128)(2,1)S(1)}, bf16[40,256]{1,0:T(8,128)(2,1)S(1)}, u32[]{:S(2)}, u32[]{:S(2)}) collective-permute-start(bf16[40,256]{1,0:T(8,128)(2,1)S(1)} %get-tuple-element.57), channel_id=1, source_target_pairs={{0,12},{4,16},{8,20},{12,24},{16,28},{20,32},{24,36},{28,40},{32,4... | collective-permute-start | bytes 61448
  765.8 16.0 %collective-permute-start.16 = (bf16[40,256]{1,0:T(8,128)(2,1)S(1)}, bf16[40,256]{1,0:T(8,128)(2,1)S(1)}, u32[]{:S(2)}, u32[]{:S(2)}) collective-permute-start(bf16[40,256]{1,0:T(8,128)(2,1)S(1)} %get-tuple-element.57), channel_id=1, source_target_pairs={{0,8},{4,12},{8,16},{12,20},{16,24},{20,28},{24,32},{28,36},{32,40... | collective-permute-start | bytes 61448
  769.5 14.1 %collective-permute-start.15 = (bf16[40,256]{1,0:T(8,128)(2,1)S(1)}, bf16[40,256]{1,0:T(8,128)(2,1)S(1)}, u32[]{:S(2)}, u32[]{:S(2)}) collective-permute-start(bf16[40,256]{1,0:T(8,128)(2,1)S(1)} %get-tuple-element.57), channel_id=1, source_target_pairs={{0,4},{4,8},{8,12},{12,16},{16,20},{20,24},{24,28},{28,32},{32,36}... | collective-permute-start | bytes 61448
  774.8 12.2 %collective-permute-start.11 = (bf16[40,256]{1,0:T(8,128)(2,1)S(1)}, bf16[40,256]{1,0:T(8,128)(2,1)S(1)}, u32[]{:S(2)}, u32[]{:S(2)}) collective-permute-start(bf16[40,256]{1,0:T(8,128)(2,1)S(1)} %get-tuple-element.56), channel_id=1, source_target_pairs={{0,4},{4,8},{8,12},{12,16},{16,20},{20,24},{24,28},{28,32},{32,36}... | collective-permute-start | bytes 61448
  777.4 13.0 %collective-permute-start.21 = (bf16[40,1728]{1,0:T(8,128)(2,1)S(1)}, bf16[40,1728]{1,0:T(8,128)(2,1)S(1)}, u32[]{:S(2)}, u32[]{:S(2)}) collective-permute-start(bf16[40,1728]{1,0:T(8,128)(2,1)S(1)} %get-tuple-element.58), channel_id=1, source_target_pairs={{0,12},{4,16},{8,20},{12,24},{16,28},{20,32},{24,36},{28,40},{32,4... | collective-permute-start | bytes 414728
  779.3 13.6 %collective-permute-start.20 = (bf16[40,1728]{1,0:T(8,128)(2,1)S(1)}, bf16[40,1728]{1,0:T(8,128)(2,1)S(1)}, u32[]{:S(2)}, u32[]{:S(2)}) collective-permute-start(bf16[40,1728]{1,0:T(8,128)(2,1)S(1)} %get-tuple-element.58), channel_id=1, source_target_pairs={{0,8},{4,12},{8,16},{12,20},{16,24},{20,28},{24,32},{28,36},{32,40... | collective-permute-start | bytes 414728
  781.8 12.6 %collective-permute-start.19 = (bf16[40,1728]{1,0:T(8,128)(2,1)S(1)}, bf16[40,1728]{1,0:T(8,128)(2,1)S(1)}, u32[]{:S(2)}, u32[]{:S(2)}) collective-permute-start(bf16[40,1728]{1,0:T(8,128)(2,1)S(1)} %get-tuple-element.58), channel_id=1, source_target_pairs={{0,4},{4,8},{8,12},{12,16},{16,20},{20,24},{24,28},{28,32},{32,36}... | collective-permute-start | bytes 414728
  783.5 13.7 %collective-permute-start.25 = (bf16[40,1728]{1,0:T(8,128)(2,1)S(1)}, bf16[40,1728]{1,0:T(8,128)(2,1)S(1)}, u32[]{:S(2)}, u32[]{:S(2)}) collective-permute-start(bf16[40,1728]{1,0:T(8,128)(2,1)S(1)} %get-tuple-element.59), channel_id=1, source_target_pairs={{0,12},{4,16},{8,20},{12,24},{16,28},{20,32},{24,36},{28,40},{32,4... | collective-permute-start | bytes 414728
  787.1 13.4 %collective-permute-start.24 = (bf16[40,1728]{1,0:T(8,128)(2,1)S(1)}, bf16[40,1728]{1,0:T(8,128)(2,1)S(1)}, u32[]{:S(2)}, u32[]{:S(2)}) collective-permute-start(bf16[40,1728]{1,0:T(8,128)(2,1)S(1)} %get-tuple-element.59), channel_id=1, source_target_pairs={{0,8},{4,12},{8,16},{12,20},{16,24},{20,28},{24,32},{28,36},{32,40... | collective-permute-start | bytes 414728
  790.4 12.4 %collective-permute-start.23 = (bf16[40,1728]{1,0:T(8,128)(2,1)S(1)}, bf16[40,1728]{1,0:T(8,128)(2,1)}, u32[]{:S(2)}, u32[]{:S(2)}) collective-permute-start(bf16[40,1728]{1,0:T(8,128)(2,1)S(1)} %get-tuple-element.59), channel_id=1, source_target_pairs={{0,4},{4,8},{8,12},{12,16},{16,20},{20,24},{24,28},{28,32},{32,36}... | collective-permute-start | bytes 414728
  792.9 12.4 %collective-permute-start.29 = (bf16[40,1728]{1,0:T(8,128)(2,1)S(1)}, bf16[40,1728]{1,0:T(8,128)(2,1)S(1)}, u32[]{:S(2)}, u32[]{:S(2)}) collective-permute-start(bf16[40,1728]{1,0:T(8,128)(2,1)S(1)} %get-tuple-element.60), channel_id=1, source_target_pairs={{0,12},{4,16},{8,20},{12,24},{16,28},{20,32},{24,36},{28,40},{32,4... | collective-permute-start | bytes 414728
  794.4 10.9 %collective-permute-start.28 = (bf16[40,1728]{1,0:T(8,128)(2,1)S(1)}, bf16[40,1728]{1,0:T(8,128)(2,1)}, u32[]{:S(2)}, u32[]{:S(2)}) collective-permute-start(bf16[40,1728]{1,0:T(8,128)(2,1)S(1)} %get-tuple-element.60), channel_id=1, source_target_pairs={{0,8},{4,12},{8,16},{12,20},{16,24},{20,28},{24,32},{28,36},{32,40... | collective-permute-start | bytes 414728
  797.3 8.6 collective-permute-start.27
  800.5 4.7 collective-permute-start.30
  802.7 155.0 %copy-start.7 = (f32[160,1152]{1,0:T(8,128)S(1)}, f32[160,1152]{1,0:T(8,128)}, u32[]{:S(2)}) copy-start(f32[160,1152]{1,0:T(8,128)} %copy-done.6) | copy-start | bytes 2211844
  (50 other events, 398.6 us)
Sparse Core Ops, SparseCore 0:
  147.6 23.1 all-gather.13
  253.2 36.2 reduce-scatter.18
  444.1 33.6 reduce-scatter.20
  482.0 25.4 all-gather.15
  526.6 36.9 reduce-scatter.22
  568.8 25.4 all-gather.17
  606.8 25.5 reduce-scatter.24
Sparse Core Ops, SparseCore 1:
  255.9 45.7 all-gather.19
  303.8 45.7 all-gather.21
  351.8 45.7 all-gather.23
